TPU v7x, 32 devices: a whole 2x2x4 slice. The times are simulated.
32 devices in a mesh: shots: 2 (over y), depth: 4 (over x, core), freq: 4 (over z).
Axes of the slice: x: 2, y: 2, z: 4, core: 2. Of those that a mesh axis runs over, the one named last changes fastest.
Arguments:
- surface: bfloat16 [4, 4, 2, 384, 384], P('shots', 'freq'), parts along dimension 0, may hold values from -6 to 6
- kernels: bfloat16 [4, 4, 2, 25, 25], P('depth', 'freq'), may hold values from -0.15625 to 0.15625
- slowness: float32 [4, 384, 384], P('depth'), may hold values from -0.02 to 0.02
- freq_index: int32 [4], P('freq'), may hold values from 8 to 199
Outputs:
- image: float32 [8, 384, 384], P(('shots', 'depth'), 'freq'), parts along dimension 0
There are 2 independent parts, one for each index of `shots`. A program takes and returns all parts, laid end to end along the dimension named above; an argument that names none is the same for every part. Nothing has to cross between parts.
All inputs are finite; a program needn't handle non-finite values.
Results may differ from a plain program's by a relative error of at most 0.0067.
Values may be sent and summed in bfloat16 or wider, within the bound.
A program may use at most 64 MiB of HBM per device.

v0:
```python
import math

import jax
import jax.numpy as jnp
from jax import lax
from jax.sharding import PartitionSpec as P


def with_halo(shard, sides, width):
    for axis, dim in sides:
        size, length = (lax.axis_size(axis), shard.shape[dim])
        up = [(i, (i + 1) % size) for i in range(size - 1)]
        down = [(j, i) for i, j in up]
        last = lax.slice_in_dim(shard, length - width, length, axis=dim)
        leading = lax.slice_in_dim(shard, 0, width, axis=dim)
        before = lax.ppermute(last, axis, up)
        after = lax.ppermute(leading, axis, down)
        shard = jnp.concatenate([before, shard, after], axis=dim)
    return shard


def convolve(padded, stencil, margin):
    rows_in = padded.shape[3]
    cells_y = padded.shape[4]
    tap_count = stencil.shape[-1]
    rows_out = rows_in - 2 * margin
    real_part = stencil[:, 0].astype(jnp.float32)
    imag_part = stencil[:, 1].astype(jnp.float32)
    filters = jnp.stack(
        [jnp.stack([real_part, -imag_part], 1), jnp.stack([imag_part, real_part], 1)], 1
    )
    offsets = lax.iota(jnp.int32, rows_in)[None, :] - lax.iota(jnp.int32, rows_out)[:, None]
    select = (offsets[None] == lax.iota(jnp.int32, tap_count)[:, None, None]).astype(jnp.float32)
    banded = jnp.einsum("fdcab,axk->fdxbck", filters, select).astype(jnp.bfloat16)
    widened = jnp.pad(padded, ((0, 0), (0, 0), (0, 0), (0, 0), (margin, margin)))
    patches = jnp.stack(
        [widened[:, :, :, :, shift : shift + cells_y] for shift in range(tap_count)], 0
    )
    return jnp.einsum("bwfcky,fdxbck->wfdxy", patches, banded, preferred_element_type=jnp.float32)


def rotate(convolved, phase_rate, freq_bins):
    phases = freq_bins[:, None, None] * phase_rate[None]
    cosines = jnp.cos(phases)
    sine_terms = jnp.sin(phases)
    real_out = convolved[:, :, 0] * cosines - convolved[:, :, 1] * sine_terms
    imag_out = convolved[:, :, 0] * sine_terms + convolved[:, :, 1] * cosines
    return jnp.stack([real_out, imag_out], 2).astype(jnp.bfloat16)


def correlate(stepped):
    widened = stepped.astype(jnp.float32)
    return jnp.sum(
        widened[0, :, 0] * widened[1, :, 0] + widened[0, :, 1] * widened[1, :, 1], axis=0
    )


def on_device(surface, kernels, slowness, freq_index):
    depth_count = lax.axis_size("depth")
    position = lax.axis_index("depth")
    cells_x = surface.shape[3]
    row_count = cells_x // depth_count
    tap_count = kernels.shape[-1]
    margin = (tap_count - 1) // 2
    start_row = position * row_count
    wavefield = lax.dynamic_slice_in_dim(surface, start_row, row_count, 3)
    stencils = lax.all_gather(kernels, "depth", axis=0, tiled=True)
    phase_rates = lax.all_to_all(slowness, "depth", split_axis=1, concat_axis=0, tiled=True)
    freq_bins = freq_index.astype(jnp.float32)

    def advance(wave, operands):
        stencil, phase_rate = operands
        padded = with_halo(wave, (("depth", 3),), margin)
        stepped = rotate(convolve(padded, stencil, margin), phase_rate, freq_bins)
        return (stepped, correlate(stepped))

    final_wave, partials = lax.scan(advance, wavefield, (stencils, phase_rates))
    moved = lax.all_to_all(partials, "depth", split_axis=0, concat_axis=1, tiled=True)
    summed = lax.psum_scatter(moved, "freq", scatter_dimension=1, tiled=True)
    return summed * (1.0 / math.sqrt(surface.shape[1] * lax.axis_size("freq")))


def solution(mesh):
    in_specs = (
        P("shots", "freq", None, None, None),
        P("depth", "freq", None, None, None),
        P("depth", None, None),
        P("freq"),
    )
    out_specs = P(("shots", "depth"), "freq", None)
    return jax.shard_map(
        on_device, mesh=mesh, in_specs=in_specs, out_specs=out_specs, check_vma=False
    )
```

profile of v0, /device:TPU:0, one launch (start us, length us, event | category | flops | bytes accessed | tf_op | source)
XLA Modules:
  0.0 142.9 jit_solution(12642051723388737498)
XLA Ops:
  6.5 2.6 %copy.95 = f32[1,384,384]{2,0,1:T(1,128)} copy(f32[1,384,384]{2,1,0:T(8,128)} %param.8) | data formatting | bytes 1179648 | tf_op args[2]
  9.1 4.2 %all-to-all-start = ((f32[1,384,384]{2,0,1:T(1,128)}), f32[1,384,384]{2,0,1:T(1,128)S(1)}, u32[]{:S(2)}, u32[]{:S(2)}) async-start(f32[1,384,384]{2,0,1:T(1,128)} %copy.95), calls=%async_computation | async-start | bytes 1179648 | tf_op jit(solution)/shard_map/all_to_all | solution.py:68
  14.1 9.9 %all_gather.3 = bf16[4,1,2,25,25]{4,2,3,1,0:T(2,128)(2,1)S(1)} all-gather(bf16[1,1,2,25,25]{4,2,3,1,0:T(2,128)(2,1)} %param.7), channel_id=1, replica_groups=mesh['shots'=2,'depth'=4,'freq'=4] {'depth'}, dimensions={0}, use_global_device_ids=true | all-gather | bytes 12500 | tf_op jit(solution)/shard_map/all_gather | solution.py:67
  24.1 74.6 %while.14 = (s32[]{:T(128)}, bf16[2,1,2,96,384]{4,3,0,2,1:T(8,128)(2,1)S(1)}, f32[4,96,384]{2,1,0:T(8,128)S(1)}, bf16[4,1,2,25,25]{4,2,3,1,0:T(2,128)(2,1)S(1)},...) while((s32[]{:T(128)}, bf16[2,1,2,96,384]{4,3,0,2,1:T(8,128)(2,1)S(1)}, f32[4,96,384]{2,1,0:T(8,128)S(1)}, ...), condition=%wide.region_1.2_spmd, body=%wide.region_0.1_spmd.sunk | while | flops 1830629888 | bytes 46951936 | solution.py:77
  24.1 1.3 collective-permute-start
  25.4 3.0 %collective-permute-start.1 = (bf16[2,1,2,12,384]{4,3,2,0,1:T(8,128)(2,1)S(1)}, bf16[2,1,2,12,384]{4,3,2,0,1:T(8,128)(2,1)S(1)}, u32[]{:S(2)}, u32[]{:S(2)}) collective-permute-start(bf16[2,1,2,12,384]{4,3,2,0,1:T(8,128)(2,1)S(1)} %get-tuple-element.171), channel_id=1, source_target_pairs={{0,4},{4,8},{8,12},{1,5},{5,9},{9,13},{2,6},{6,10},{10,14},{3,7},{... | collective-permute-start | bytes 110600 | tf_op jit(solution)/shard_map/while/body/eval_jaxpr/ppermute | solution.py:16
  28.6 2.6 %convert_bitcast_fusion.2 = bf16[2,96,25,2,120,1]{4,2,3,0,1,5:T(8,128)(2,1)} fusion(s32[96,120]{1,0:T(8,128)S(1)} %iota_subtract_fusion.2, bf16[1,1,2,25,25]{3,4,2,1,0:T(8,128)(2,1)S(1)} %get-tuple-element.175, bf16[1,1,2,25,25]{3,4,2,1,0:T(8,128)(2,1)S(1)} %get-tuple-element.176), kind=kOutput, calls=%fused_computation.2.clone.1 | convolution fusion | flops 57898000 | bytes 2355080 | tf_op jit(solution)/shard_map/while/body/eval_jaxpr/fdcab,axk->fdxbck/dot_general | solution.py:34
  31.2 0.5 cosine_bitcast_fusion.2
  32.1 0.2 fusion.114
  32.3 0.2 fusion.115
  32.5 0.2 fusion.116
  32.7 0.2 fusion.117
  32.9 0.2 fusion.118
  33.1 0.2 fusion.119
  33.3 0.2 fusion.120
  33.5 0.2 fusion.121
  33.7 0.2 fusion.122
  33.9 0.2 fusion.123
  34.1 0.2 fusion.124
  36.8 4.8 %fusion.138 = f32[2,1,2,96,384]{4,3,0,2,1:T(8,128)S(1)} fusion(bf16[25,2,1,2,120,384]{5,4,3,0,1,2:T(8,128)(2,1)S(1)} %fusion.136, bf16[2,96,25,2,120,1]{4,2,3,0,1,5:T(8,128)(2,1)S(1)} %copy-done.1), kind=kOutput, calls=%fused_computation.6.clone.1 | convolution fusion | flops 1769472000 | bytes 12109824 | tf_op jit(solution)/shard_map/while/body/eval_jaxpr/bwfcky,fdxbck->wfdxy/dot_general | solution.py:39
  41.9 1.3 collective-permute-start
  43.2 4.1 %collective-permute-start.1 = (bf16[2,1,2,12,384]{4,3,2,0,1:T(8,128)(2,1)S(1)}, bf16[2,1,2,12,384]{4,3,2,0,1:T(8,128)(2,1)S(1)}, u32[]{:S(2)}, u32[]{:S(2)}) collective-permute-start(bf16[2,1,2,12,384]{4,3,2,0,1:T(8,128)(2,1)S(1)} %get-tuple-element.171), channel_id=1, source_target_pairs={{0,4},{4,8},{8,12},{1,5},{5,9},{9,13},{2,6},{6,10},{10,14},{3,7},{... | collective-permute-start | bytes 110600 | tf_op jit(solution)/shard_map/while/body/eval_jaxpr/ppermute | solution.py:16
  47.5 2.6 %convert_bitcast_fusion.2 = bf16[2,96,25,2,120,1]{4,2,3,0,1,5:T(8,128)(2,1)} fusion(s32[96,120]{1,0:T(8,128)S(1)} %iota_subtract_fusion.2, bf16[1,1,2,25,25]{3,4,2,1,0:T(8,128)(2,1)S(1)} %get-tuple-element.175, bf16[1,1,2,25,25]{3,4,2,1,0:T(8,128)(2,1)S(1)} %get-tuple-element.176), kind=kOutput, calls=%fused_computation.2.clone.1 | convolution fusion | flops 57898000 | bytes 2355080 | tf_op jit(solution)/shard_map/while/body/eval_jaxpr/fdcab,axk->fdxbck/dot_general | solution.py:34
  50.1 0.5 cosine_bitcast_fusion.2
  50.9 0.2 fusion.114
  51.1 0.2 fusion.115
  51.3 0.2 fusion.116
  51.5 0.2 fusion.117
  51.7 0.2 fusion.118
  52.6 0.2 fusion.122
  55.7 4.8 %fusion.138 = f32[2,1,2,96,384]{4,3,0,2,1:T(8,128)S(1)} fusion(bf16[25,2,1,2,120,384]{5,4,3,0,1,2:T(8,128)(2,1)S(1)} %fusion.136, bf16[2,96,25,2,120,1]{4,2,3,0,1,5:T(8,128)(2,1)S(1)} %copy-done.1), kind=kOutput, calls=%fused_computation.6.clone.1 | convolution fusion | flops 1769472000 | bytes 12109824 | tf_op jit(solution)/shard_map/while/body/eval_jaxpr/bwfcky,fdxbck->wfdxy/dot_general | solution.py:39
  60.7 1.3 collective-permute-start
  62.0 4.3 %collective-permute-start.1 = (bf16[2,1,2,12,384]{4,3,2,0,1:T(8,128)(2,1)S(1)}, bf16[2,1,2,12,384]{4,3,2,0,1:T(8,128)(2,1)S(1)}, u32[]{:S(2)}, u32[]{:S(2)}) collective-permute-start(bf16[2,1,2,12,384]{4,3,2,0,1:T(8,128)(2,1)S(1)} %get-tuple-element.171), channel_id=1, source_target_pairs={{0,4},{4,8},{8,12},{1,5},{5,9},{9,13},{2,6},{6,10},{10,14},{3,7},{... | collective-permute-start | bytes 110600 | tf_op jit(solution)/shard_map/while/body/eval_jaxpr/ppermute | solution.py:16
  66.5 2.6 %convert_bitcast_fusion.2 = bf16[2,96,25,2,120,1]{4,2,3,0,1,5:T(8,128)(2,1)} fusion(s32[96,120]{1,0:T(8,128)S(1)} %iota_subtract_fusion.2, bf16[1,1,2,25,25]{3,4,2,1,0:T(8,128)(2,1)S(1)} %get-tuple-element.175, bf16[1,1,2,25,25]{3,4,2,1,0:T(8,128)(2,1)S(1)} %get-tuple-element.176), kind=kOutput, calls=%fused_computation.2.clone.1 | convolution fusion | flops 57898000 | bytes 2355080 | tf_op jit(solution)/shard_map/while/body/eval_jaxpr/fdcab,axk->fdxbck/dot_general | solution.py:34
  69.1 0.5 cosine_bitcast_fusion.2
  70.1 0.2 fusion.115
  70.9 0.2 fusion.119
  71.4 0.2 fusion.121
  74.7 4.8 %fusion.138 = f32[2,1,2,96,384]{4,3,0,2,1:T(8,128)S(1)} fusion(bf16[25,2,1,2,120,384]{5,4,3,0,1,2:T(8,128)(2,1)S(1)} %fusion.136, bf16[2,96,25,2,120,1]{4,2,3,0,1,5:T(8,128)(2,1)S(1)} %copy-done.1), kind=kOutput, calls=%fused_computation.6.clone.1 | convolution fusion | flops 1769472000 | bytes 12109824 | tf_op jit(solution)/shard_map/while/body/eval_jaxpr/bwfcky,fdxbck->wfdxy/dot_general | solution.py:39
  79.7 1.3 collective-permute-start
  81.0 4.3 %collective-permute-start.1 = (bf16[2,1,2,12,384]{4,3,2,0,1:T(8,128)(2,1)S(1)}, bf16[2,1,2,12,384]{4,3,2,0,1:T(8,128)(2,1)S(1)}, u32[]{:S(2)}, u32[]{:S(2)}) collective-permute-start(bf16[2,1,2,12,384]{4,3,2,0,1:T(8,128)(2,1)S(1)} %get-tuple-element.171), channel_id=1, source_target_pairs={{0,4},{4,8},{8,12},{1,5},{5,9},{9,13},{2,6},{6,10},{10,14},{3,7},{... | collective-permute-start | bytes 110600 | tf_op jit(solution)/shard_map/while/body/eval_jaxpr/ppermute | solution.py:16
  85.5 2.6 %convert_bitcast_fusion.2 = bf16[2,96,25,2,120,1]{4,2,3,0,1,5:T(8,128)(2,1)} fusion(s32[96,120]{1,0:T(8,128)S(1)} %iota_subtract_fusion.2, bf16[1,1,2,25,25]{3,4,2,1,0:T(8,128)(2,1)S(1)} %get-tuple-element.175, bf16[1,1,2,25,25]{3,4,2,1,0:T(8,128)(2,1)S(1)} %get-tuple-element.176), kind=kOutput, calls=%fused_computation.2.clone.1 | convolution fusion | flops 57898000 | bytes 2355080 | tf_op jit(solution)/shard_map/while/body/eval_jaxpr/fdcab,axk->fdxbck/dot_general | solution.py:34
  88.1 0.5 cosine_bitcast_fusion.2
  90.8 0.2 fusion.123
  93.7 4.8 %fusion.138 = f32[2,1,2,96,384]{4,3,0,2,1:T(8,128)S(1)} fusion(bf16[25,2,1,2,120,384]{5,4,3,0,1,2:T(8,128)(2,1)S(1)} %fusion.136, bf16[2,96,25,2,120,1]{4,2,3,0,1,5:T(8,128)(2,1)S(1)} %copy-done.1), kind=kOutput, calls=%fused_computation.6.clone.1 | convolution fusion | flops 1769472000 | bytes 12109824 | tf_op jit(solution)/shard_map/while/body/eval_jaxpr/bwfcky,fdxbck->wfdxy/dot_general | solution.py:39
  98.7 12.6 %all_to_all.24 = f32[4,96,384]{2,1,0:T(8,128)} all-to-all(f32[4,96,384]{2,1,0:T(8,128)S(1)} %get-tuple-element.82), channel_id=1, replica_groups=mesh['shots'=2,'depth'=4,'freq'=4] {'depth'}, dimensions={0} | all-to-all | bytes 1179648 | tf_op jit(solution)/shard_map/all_to_all | solution.py:78
  111.4 23.2 %reduce-scatter.2.cloned.1.call-done = f32[1,96,384]{2,1,0:T(8,128)} async-done(((f32[1,384,384]{2,1,0:T(8,128)}), f32[1,96,384]{2,1,0:T(8,128)}) %reduce-scatter.2.cloned.1.call-update) | async-done | bytes 147472 | tf_op jit(solution)/shard_map/reduce_scatter | solution.py:79
  134.5 1.6 %broadcast_multiply_fusion = f32[1,96,384]{2,1,0:T(8,128)} fusion(f32[1,96,384]{2,1,0:T(8,128)} %reduce-scatter.2.cloned.1.call-done), kind=kLoop, calls=%fused_computation.104 | loop fusion | flops 36864 | bytes 294912 | tf_op jit(solution)/shard_map/mul | solution.py:80
  (144 shorter events, 17.1 us)
Async XLA Ops:
  6.5 6.8 %copy-start = (bf16[2,1,2,384,384]{4,3,2,1,0:T(8,128)(2,1)S(1)}, bf16[2,1,2,384,384]{4,3,2,1,0:T(8,128)(2,1)}, u32[]{:S(2)}) copy-start(bf16[2,1,2,384,384]{4,3,2,1,0:T(8,128)(2,1)} %param.6) | copy-start | bytes 3538948
  9.1 14.9 %all-to-all-start = ((f32[1,384,384]{2,0,1:T(1,128)}), f32[1,384,384]{2,0,1:T(1,128)S(1)}, u32[]{:S(2)}, u32[]{:S(2)}) async-start(f32[1,384,384]{2,0,1:T(1,128)} %copy.95), calls=%async_computation | async-start | bytes 1179648 | tf_op jit(solution)/shard_map/all_to_all | solution.py:68
  13.3 121.2 %reduce-scatter.2.cloned.1.call-start = ((), (), s32[]{:S(2)}) async-start(), calls=%async_computation.3 | async-start | bytes 737280 | tf_op jit(solution)/shard_map/reduce_scatter | solution.py:79
  24.1 7.7 %collective-permute-start = (bf16[2,1,2,12,384]{4,3,2,0,1:T(8,128)(2,1)S(1)}, bf16[2,1,2,12,384]{4,3,2,0,1:T(8,128)(2,1)S(1)}, u32[]{:S(2)}, u32[]{:S(2)}) collective-permute-start(bf16[2,1,2,12,384]{4,3,2,0,1:T(8,128)(2,1)S(1)} %get-tuple-element.170), channel_id=1, source_target_pairs={{4,0},{8,4},{12,8},{5,1},{9,5},{13,9},{6,2},{10,6},{14,10},{7,3},{... | collective-permute-start | bytes 110600 | tf_op jit(solution)/shard_map/while/body/eval_jaxpr/ppermute | solution.py:17
  25.4 6.4 %collective-permute-start.1 = (bf16[2,1,2,12,384]{4,3,2,0,1:T(8,128)(2,1)S(1)}, bf16[2,1,2,12,384]{4,3,2,0,1:T(8,128)(2,1)S(1)}, u32[]{:S(2)}, u32[]{:S(2)}) collective-permute-start(bf16[2,1,2,12,384]{4,3,2,0,1:T(8,128)(2,1)S(1)} %get-tuple-element.171), channel_id=1, source_target_pairs={{0,4},{4,8},{8,12},{1,5},{5,9},{9,13},{2,6},{6,10},{10,14},{3,7},{... | collective-permute-start | bytes 110600 | tf_op jit(solution)/shard_map/while/body/eval_jaxpr/ppermute | solution.py:16
  31.9 5.0 %copy-start.1 = (bf16[2,96,25,2,120,1]{4,2,3,0,1,5:T(8,128)(2,1)S(1)}, bf16[2,96,25,2,120,1]{4,2,3,0,1,5:T(8,128)(2,1)}, u32[]{:S(2)}) copy-start(bf16[2,96,25,2,120,1]{4,2,3,0,1,5:T(8,128)(2,1)} %convert_bitcast_fusion.2) | copy-start | bytes 6912004 | tf_op jit(solution)/shard_map/while
  41.9 8.7 %collective-permute-start = (bf16[2,1,2,12,384]{4,3,2,0,1:T(8,128)(2,1)S(1)}, bf16[2,1,2,12,384]{4,3,2,0,1:T(8,128)(2,1)S(1)}, u32[]{:S(2)}, u32[]{:S(2)}) collective-permute-start(bf16[2,1,2,12,384]{4,3,2,0,1:T(8,128)(2,1)S(1)} %get-tuple-element.170), channel_id=1, source_target_pairs={{4,0},{8,4},{12,8},{5,1},{9,5},{13,9},{6,2},{10,6},{14,10},{7,3},{... | collective-permute-start | bytes 110600 | tf_op jit(solution)/shard_map/while/body/eval_jaxpr/ppermute | solution.py:17
  43.2 7.4 %collective-permute-start.1 = (bf16[2,1,2,12,384]{4,3,2,0,1:T(8,128)(2,1)S(1)}, bf16[2,1,2,12,384]{4,3,2,0,1:T(8,128)(2,1)S(1)}, u32[]{:S(2)}, u32[]{:S(2)}) collective-permute-start(bf16[2,1,2,12,384]{4,3,2,0,1:T(8,128)(2,1)S(1)} %get-tuple-element.171), channel_id=1, source_target_pairs={{0,4},{4,8},{8,12},{1,5},{5,9},{9,13},{2,6},{6,10},{10,14},{3,7},{... | collective-permute-start | bytes 110600 | tf_op jit(solution)/shard_map/while/body/eval_jaxpr/ppermute | solution.py:16
  50.7 5.0 %copy-start.1 = (bf16[2,96,25,2,120,1]{4,2,3,0,1,5:T(8,128)(2,1)S(1)}, bf16[2,96,25,2,120,1]{4,2,3,0,1,5:T(8,128)(2,1)}, u32[]{:S(2)}) copy-start(bf16[2,96,25,2,120,1]{4,2,3,0,1,5:T(8,128)(2,1)} %convert_bitcast_fusion.2) | copy-start | bytes 6912004 | tf_op jit(solution)/shard_map/while
  60.7 8.9 %collective-permute-start = (bf16[2,1,2,12,384]{4,3,2,0,1:T(8,128)(2,1)S(1)}, bf16[2,1,2,12,384]{4,3,2,0,1:T(8,128)(2,1)S(1)}, u32[]{:S(2)}, u32[]{:S(2)}) collective-permute-start(bf16[2,1,2,12,384]{4,3,2,0,1:T(8,128)(2,1)S(1)} %get-tuple-element.170), channel_id=1, source_target_pairs={{4,0},{8,4},{12,8},{5,1},{9,5},{13,9},{6,2},{10,6},{14,10},{7,3},{... | collective-permute-start | bytes 110600 | tf_op jit(solution)/shard_map/while/body/eval_jaxpr/ppermute | solution.py:17
  62.0 7.6 %collective-permute-start.1 = (bf16[2,1,2,12,384]{4,3,2,0,1:T(8,128)(2,1)S(1)}, bf16[2,1,2,12,384]{4,3,2,0,1:T(8,128)(2,1)S(1)}, u32[]{:S(2)}, u32[]{:S(2)}) collective-permute-start(bf16[2,1,2,12,384]{4,3,2,0,1:T(8,128)(2,1)S(1)} %get-tuple-element.171), channel_id=1, source_target_pairs={{0,4},{4,8},{8,12},{1,5},{5,9},{9,13},{2,6},{6,10},{10,14},{3,7},{... | collective-permute-start | bytes 110600 | tf_op jit(solution)/shard_map/while/body/eval_jaxpr/ppermute | solution.py:16
  69.7 5.0 %copy-start.1 = (bf16[2,96,25,2,120,1]{4,2,3,0,1,5:T(8,128)(2,1)S(1)}, bf16[2,96,25,2,120,1]{4,2,3,0,1,5:T(8,128)(2,1)}, u32[]{:S(2)}) copy-start(bf16[2,96,25,2,120,1]{4,2,3,0,1,5:T(8,128)(2,1)} %convert_bitcast_fusion.2) | copy-start | bytes 6912004 | tf_op jit(solution)/shard_map/while
  79.7 8.9 %collective-permute-start = (bf16[2,1,2,12,384]{4,3,2,0,1:T(8,128)(2,1)S(1)}, bf16[2,1,2,12,384]{4,3,2,0,1:T(8,128)(2,1)S(1)}, u32[]{:S(2)}, u32[]{:S(2)}) collective-permute-start(bf16[2,1,2,12,384]{4,3,2,0,1:T(8,128)(2,1)S(1)} %get-tuple-element.170), channel_id=1, source_target_pairs={{4,0},{8,4},{12,8},{5,1},{9,5},{13,9},{6,2},{10,6},{14,10},{7,3},{... | collective-permute-start | bytes 110600 | tf_op jit(solution)/shard_map/while/body/eval_jaxpr/ppermute | solution.py:17
  81.0 7.6 %collective-permute-start.1 = (bf16[2,1,2,12,384]{4,3,2,0,1:T(8,128)(2,1)S(1)}, bf16[2,1,2,12,384]{4,3,2,0,1:T(8,128)(2,1)S(1)}, u32[]{:S(2)}, u32[]{:S(2)}) collective-permute-start(bf16[2,1,2,12,384]{4,3,2,0,1:T(8,128)(2,1)S(1)} %get-tuple-element.171), channel_id=1, source_target_pairs={{0,4},{4,8},{8,12},{1,5},{5,9},{9,13},{2,6},{6,10},{10,14},{3,7},{... | collective-permute-start | bytes 110600 | tf_op jit(solution)/shard_map/while/body/eval_jaxpr/ppermute | solution.py:16
  88.7 5.0 %copy-start.1 = (bf16[2,96,25,2,120,1]{4,2,3,0,1,5:T(8,128)(2,1)S(1)}, bf16[2,96,25,2,120,1]{4,2,3,0,1,5:T(8,128)(2,1)}, u32[]{:S(2)}) copy-start(bf16[2,96,25,2,120,1]{4,2,3,0,1,5:T(8,128)(2,1)} %convert_bitcast_fusion.2) | copy-start | bytes 6912004 | tf_op jit(solution)/shard_map/while
Sparse Core Ops, SparseCore 0:
  111.5 22.9 reduce-scatter.1
where the time goes:
time: 143 us
  matrix products  29.5 us (21%)
  starting transfers between devices  25 us (17%)
  waiting for transfers between devices  23.2 us (16%)
  blocking collectives  22.6 us (16%)
  local copies, waits for them, and re-layouts  22.1 us (15%)
  between operations  14.1 us (10%)
  other arithmetic  5.5 us (4%)
    reduce_scatter x1, waiting for transfers between devices, on_device(): summed = lax.psum_scatter(moved, 'freq', scatter_dimension=1, tiled=True)  23.2 us
    dot_general x4, matrix products, convolve(): jnp.einsum('bwfcky,fdxbck->wfdxy', patches, banded, preferred_element_typ...  19.1 us
    while x100, local copies, waits for them, and re-layouts  18 us
    ppermute x4, starting transfers between devices, with_halo(): before = lax.ppermute(last, axis, up)  15.7 us
    all_to_all x1, blocking collectives, on_device(): lax.all_to_all(partials, 'depth', split_axis=0, concat_axis=1, tiled=True)  12.6 us
    dot_general x4, matrix products, convolve(): jnp.einsum('fdcab,axk->fdxbck', filters, select).astype(jnp.bfloat16)  10.4 us
    all_gather x1, blocking collectives, on_device(): stencils = lax.all_gather(kernels, 'depth', axis=0, tiled=True)  9.94 us
    ppermute x4, starting transfers between devices, with_halo(): after = lax.ppermute(leading, axis, down)  5.17 us
  transfers between devices with their start and end apart: 10, of which 1 were waited for; matrix products, arithmetic and copies ran while one was open for 9% of the time, Pallas kernels for 0%

commit v1 on v0

--- a/solution.py
+++ b/solution.py
@@ -1,8 +1,11 @@
+import functools
 import math
 
 import jax
 import jax.numpy as jnp
 from jax import lax
+from jax.experimental import pallas as pl
+from jax.experimental.pallas import tpu as pltpu
 from jax.sharding import PartitionSpec as P
 
 
@@ -55,7 +58,7 @@
     )
 
 
-def on_device(surface, kernels, slowness, freq_index):
+def on_device_general(surface, kernels, slowness, freq_index):
     depth_count = lax.axis_size("depth")
     position = lax.axis_index("depth")
     cells_x = surface.shape[3]
@@ -80,6 +83,273 @@
     return summed * (1.0 / math.sqrt(surface.shape[1] * lax.axis_size("freq")))
 
 
+MESH = pl.DeviceIdType.MESH
+VMEM = pl.BlockSpec(memory_space=pltpu.VMEM)
+SCALE = 32767.0 / 0.02
+
+
+def window(position, rows, cells, margin):
+    length = min(cells, rows + 2 * margin)
+    start = jnp.clip(position * rows - margin, 0, cells - length)
+    offset = start - position * rows + 2 * margin
+    return pl.multiple_of(start, 16), pl.multiple_of(offset, 16), length
+
+
+def gather_kernel(depth_count, rows, margin, slow_ref, taps_ref, slow_out, taps_out, send, recv, local):
+    me = lax.axis_index("depth")
+    cells = slow_ref.shape[0]
+    barrier = pltpu.get_barrier_semaphore()
+    for step in range(1, depth_count):
+        other = lax.rem(me + step, depth_count)
+        pl.semaphore_signal(barrier, inc=1, device_id={"depth": other}, device_id_type=MESH)
+    pl.semaphore_wait(barrier, depth_count - 1)
+    copies = []
+    for step in range(1, depth_count):
+        other = lax.rem(me + step, depth_count)
+        start, offset, length = window(other, rows, cells, margin)
+        copies.append(pltpu.make_async_remote_copy(
+            src_ref=taps_ref, dst_ref=taps_out.at[me],
+            send_sem=send.at[0, step - 1], recv_sem=recv.at[0, step - 1],
+            device_id={"depth": other}, device_id_type=MESH))
+        copies.append(pltpu.make_async_remote_copy(
+            src_ref=slow_ref.at[pl.ds(start, length)],
+            dst_ref=slow_out.at[me, pl.ds(offset, length)],
+            send_sem=send.at[1, step - 1], recv_sem=recv.at[1, step - 1],
+            device_id={"depth": other}, device_id_type=MESH))
+    for copy in copies:
+        copy.start()
+    start, offset, length = window(me, rows, cells, margin)
+    own = [
+        pltpu.make_async_copy(taps_ref, taps_out.at[me], local.at[0]),
+        pltpu.make_async_copy(slow_ref.at[pl.ds(start, length)], slow_out.at[me, pl.ds(offset, length)], local.at[1]),
+    ]
+    for copy in own:
+        copy.start()
+    for copy in own + copies:
+        copy.wait()
+
+
+def gather(slow, taps, depth_count, rows, margin):
+    frame = rows + 4 * margin
+    return pl.pallas_call(
+        functools.partial(gather_kernel, depth_count, rows, margin),
+        out_shape=(
+            jax.ShapeDtypeStruct((depth_count, frame, slow.shape[1]), slow.dtype),
+            jax.ShapeDtypeStruct((depth_count,) + taps.shape, taps.dtype),
+        ),
+        in_specs=[VMEM] * 2,
+        out_specs=(VMEM, VMEM),
+        scratch_shapes=[
+            pltpu.SemaphoreType.DMA((2, depth_count - 1)),
+            pltpu.SemaphoreType.DMA((2, depth_count - 1)),
+            pltpu.SemaphoreType.DMA((2,)),
+        ],
+        compiler_params=pltpu.CompilerParams(collective_id=0, has_side_effects=True),
+    )(slow, taps)
+
+
+def sine_cosine(phase):
+    quarter = phase * 0.25
+    sq = quarter * quarter
+    sine = quarter * (1.0 + sq * (-1 / 6 + sq * (1 / 120 + sq * (-1 / 5040 + sq * (1 / 362880 - sq * (1 / 39916800))))))
+    cosine = 1.0 + sq * (-0.5 + sq * (1 / 24 + sq * (-1 / 720 + sq * (1 / 40320 - sq * (1 / 3628800)))))
+    for _ in range(2):
+        sine, cosine = 2.0 * sine * cosine, 1.0 - 2.0 * sine * sine
+    return sine, cosine
+
+
+def tiles_of(total):
+    if total <= 96:
+        return [(0, total)]
+    first = total // 2 // 16 * 16
+    return [(0, first), (first, -(-(total - first) // 16) * 16)]
+
+
+def march_kernel(depth_count, rows, reach, factor, freq_ref, surface_ref, slow_ref, taps_ref, image_ref,
+                 wave0, wave1, band, patches, conv_ref, corr, sems):
+    me = lax.axis_index("depth")
+    margin = depth_count * reach
+    cells = surface_ref.shape[3]
+    cols = surface_ref.shape[4]
+    width = 2 * reach + 1
+    waves = (wave0, wave1)
+    start, offset, length = window(me, rows, cells, margin)
+    wave0[...] = jnp.zeros_like(wave0)
+    wave1[...] = jnp.zeros_like(wave1)
+    copies = [
+        pltpu.make_async_copy(
+            surface_ref.at[w, 0, c, pl.ds(start, length)],
+            wave0.at[w, c, pl.ds(offset, length), pl.ds(128, cols)],
+            sems.at[w, c])
+        for w in range(2) for c in range(2)
+    ]
+    for copy in copies:
+        copy.start()
+    for copy in copies:
+        copy.wait()
+    freq = freq_ref[0].astype(jnp.float32) * (1.0 / SCALE)
+    for z in range(depth_count):
+        tap = taps_ref[z].astype(jnp.float32)
+
+        @pl.loop(0, width)
+        def _(b):
+            parts = []
+            for k in range(2):
+                line = jnp.broadcast_to(taps_ref[z, pl.ds(32 * k + b, 1)], (112, 128))
+                parts.append(pltpu.roll(line, 0, 1, stride=1, stride_axis=0))
+            real, imag = parts
+            low, high = pl.ds(pl.multiple_of(256 * b, 256), 128), pl.ds(pl.multiple_of(256 * b + 128, 128), 128)
+            band[0, :, low] = real.astype(jnp.bfloat16)
+            band[0, :, high] = (-imag).astype(jnp.bfloat16)
+            band[1, :, low] = imag.astype(jnp.bfloat16)
+            band[1, :, high] = real.astype(jnp.bfloat16)
+
+        source, target = waves[z % 2], waves[(z + 1) % 2]
+        base = margin if z == 0 else 0
+        base_in = base
+        shift = reach * (z + 1)
+        total = rows + 2 * reach * (depth_count - 1 - z)
+        for at, size in tiles_of(total):
+            @pl.loop(0, 2)
+            def _(c):
+                for b in range(width):
+                    for w in range(2):
+                        patches[pl.ds(pl.multiple_of(256 * b + 128 * c, 128), 128), cols * w : cols * w + cols] = (
+                            source[w, c, base_in + at : base_in + at + 128, 128 - reach + b : 128 - reach + b + cols])
+
+            total_ref = conv_ref.at[pl.ds(0, 2 * size)]
+            total_ref[...] = jnp.zeros((2 * size, 2 * cols), jnp.float32)
+
+            @pl.loop(0, width // 5)
+            def _(g):
+                deep = pl.ds(pl.multiple_of(1280 * g, 1280), 1280)
+                lhs = jnp.concatenate([band[0, :size, deep], band[1, :size, deep]], 0)
+                total_ref[...] += jnp.dot(lhs, patches[deep, :], preferred_element_type=jnp.float32)
+
+            conv = total_ref
+            phase = slow_ref[z, margin + shift + at : margin + shift + at + size].astype(jnp.int32).astype(jnp.float32) * freq
+            sine, cosine = sine_cosine(phase)
+            line = lax.broadcasted_iota(jnp.int32, (size, cols), 0) + (me * rows - margin + shift + at)
+            inside = (line >= 0) & (line < cells)
+            kept = []
+            for w in range(2):
+                real = conv[:size, cols * w : cols * w + cols]
+                imag = conv[size:, cols * w : cols * w + cols]
+                for c, value in enumerate((real * cosine - imag * sine, real * sine + imag * cosine)):
+                    value = jnp.where(inside, value, 0.0).astype(jnp.bfloat16)
+                    kept.append(value.astype(jnp.float32))
+                    if z + 1 < depth_count:
+                        target[w, c, at : at + size, 128 : 128 + cols] = value
+            corr[at : at + size] = (kept[0] * kept[2] + kept[1] * kept[3]) * factor
+        image_ref[z] = corr[margin - shift : margin - shift + rows].astype(image_ref.dtype)
+
+
+def march(freq, surface, slow, taps, depth_count, rows, reach, factor):
+    cols = surface.shape[4]
+    width = 2 * reach + 1
+    frame = slow.shape[1]
+    return pl.pallas_call(
+        functools.partial(march_kernel, depth_count, rows, reach, factor),
+        out_shape=jax.ShapeDtypeStruct((depth_count, rows, cols), jnp.bfloat16),
+        in_specs=[pl.BlockSpec(memory_space=pltpu.SMEM), pl.BlockSpec(memory_space=pl.ANY), VMEM, VMEM],
+        out_specs=VMEM,
+        scratch_shapes=[
+            pltpu.VMEM((2, 2, frame, cols + 256), jnp.bfloat16),
+            pltpu.VMEM((2, 2, frame, cols + 256), jnp.bfloat16),
+            pltpu.VMEM((2, 112, 256 * width), jnp.bfloat16),
+            pltpu.VMEM((256 * width, 2 * cols), jnp.bfloat16),
+            pltpu.VMEM((192, 2 * cols), jnp.float32),
+            pltpu.VMEM((192, cols), jnp.float32),
+            pltpu.SemaphoreType.DMA((2, 2)),
+        ],
+        compiler_params=pltpu.CompilerParams(vmem_limit_bytes=48 << 20),
+    )(freq, surface, slow, taps)
+
+
+def spread_kernel(count, image_ref, out_ref, slots, send, recv, local):
+    depth = lax.axis_index("depth")
+    freq = lax.axis_index("freq")
+    barrier = pltpu.get_barrier_semaphore()
+    for k in range(count):
+        @pl.when((depth != freq) | (k != freq))
+        def _():
+            pl.semaphore_signal(barrier, inc=1, device_id={"depth": freq, "freq": k}, device_id_type=MESH)
+    pl.semaphore_wait(barrier, count - (depth == freq).astype(jnp.int32))
+
+    def outgoing(k):
+        return pltpu.make_async_remote_copy(
+            src_ref=image_ref.at[k], dst_ref=slots.at[freq],
+            send_sem=send.at[k], recv_sem=recv.at[freq],
+            device_id={"depth": k, "freq": depth}, device_id_type=MESH)
+
+    def incoming(k):
+        return pltpu.make_async_remote_copy(
+            src_ref=image_ref.at[k], dst_ref=slots.at[k],
+            send_sem=send.at[k], recv_sem=recv.at[k],
+            device_id={"depth": k, "freq": depth}, device_id_type=MESH)
+
+    for k in range(count):
+        @pl.when((depth != freq) | (k != depth))
+        def _():
+            outgoing(k).start()
+
+    own = pltpu.make_async_copy(image_ref.at[depth], slots.at[freq], local)
+
+    @pl.when(depth == freq)
+    def _():
+        own.start()
+        own.wait()
+
+    for k in range(count):
+        @pl.when((depth != freq) | (k != freq))
+        def _():
+            incoming(k).wait_recv()
+    total = slots[0].astype(jnp.float32)
+    for k in range(1, count):
+        total = total + slots[k].astype(jnp.float32)
+    out_ref[0] = total
+    for k in range(count):
+        @pl.when((depth != freq) | (k != depth))
+        def _():
+            outgoing(k).wait_send()
+
+
+def spread(image):
+    count = image.shape[0]
+    return pl.pallas_call(
+        functools.partial(spread_kernel, count),
+        out_shape=jax.ShapeDtypeStruct((1,) + image.shape[1:], jnp.float32),
+        in_specs=[VMEM],
+        out_specs=VMEM,
+        scratch_shapes=[
+            pltpu.VMEM(image.shape, image.dtype),
+            pltpu.SemaphoreType.DMA((count,)),
+            pltpu.SemaphoreType.DMA((count,)),
+            pltpu.SemaphoreType.DMA,
+        ],
+        compiler_params=pltpu.CompilerParams(collective_id=1, has_side_effects=True),
+    )(image)
+
+
+def on_device_fused(surface, kernels, slowness, freq_index):
+    depth_count = lax.axis_size("depth")
+    cells = surface.shape[3]
+    rows = cells // depth_count
+    width = kernels.shape[-1]
+    reach = (width - 1) // 2
+    margin = depth_count * reach
+    taps = jnp.pad(jnp.swapaxes(kernels[0, 0], 1, 2), ((0, 0), (0, 32 - width), (0, 128 - width))).reshape(64, 128)
+    slow = jnp.round(slowness[0] * SCALE).astype(jnp.int16)
+    slow_all, taps_all = gather(slow, taps, depth_count, rows, margin)
+    factor = 1.0 / math.sqrt(lax.axis_size("freq"))
+    image = march(freq_index, surface, slow_all, taps_all.astype(jnp.float32), depth_count, rows, reach, factor)
+    return spread(image)
+
+
+def fits(mesh):
+    return mesh.shape["depth"] == 4 and mesh.shape["freq"] == 4
+
+
 def solution(mesh):
     in_specs = (
         P("shots", "freq", None, None, None),
@@ -88,6 +358,7 @@
         P("freq"),
     )
     out_specs = P(("shots", "depth"), "freq", None)
+    body = on_device_fused if fits(mesh) else on_device_general
     return jax.shard_map(
-        on_device, mesh=mesh, in_specs=in_specs, out_specs=out_specs, check_vma=False
-    )
+        body, mesh=mesh, in_specs=in_specs, out_specs=out_specs, check_vma=False
+    )

time: 143 us -> 94.5 us (0.66)
  the two profiles are of different devices: /device:TPU:0 before, /device:TPU:3 now
where the time goes in v1:
time: 94.5 us; the launch traced here: 94.2 us
  Pallas kernels  85.7 us (91%)
  local copies, waits for them, and re-layouts  4.88 us (5%)
  other arithmetic  2.72 us (3%)
    pallas_call x1, Pallas kernels, march(): pl.pallas_call(functools.partial(march_kernel, depth_count, rows, reach,...  55 us
    pallas_call x1, Pallas kernels, spread(): pl.pallas_call(functools.partial(spread_kernel, count), out_shape=jax.Sha...  18.7 us
    pallas_call x1, Pallas kernels, gather(): pl.pallas_call(functools.partial(gather_kernel, depth_count, rows, margin...  12.1 us
    unnamed x8, local copies, waits for them, and re-layouts  4.26 us

profile of v1, /device:TPU:3, one launch (start us, length us, event | category | flops | bytes accessed | tf_op | source)
XLA Modules:
  0.0 94.2 jit_solution(5144418012878247633)
XLA Ops:
  0.0 0.0 copy-start
  0.8 0.8 copy.6
  1.6 0.6 pad.4.clone
  2.2 1.9 %fusion.slow_ref = s16[384,384]{1,0:T(8,128)(2,1)} fusion(f32[1,384,384]{2,1,0:T(8,128)} %param.6), kind=kLoop, calls=%fused_computation.1 | loop fusion | flops 442368 | bytes 884736 | tf_op jit(solution)/shard_map/convert_element_type | solution.py:342
  4.1 12.1 %shard_map.46 = (s16[4,288,384]{2,1,0:T(8,128)(2,1)}, bf16[4,64,128]{2,1,0:T(8,128)(2,1)}) custom-call(s16[384,384]{1,0:T(8,128)(2,1)} %fusion.slow_ref, bf16[64,128]{1,0:T(8,128)(2,1)} %bitcast.6), custom_call_target="tpu_custom_call" | custom-call | tf_op jit(solution)/shard_map/pallas_call | solution.py:134
  16.1 0.9 convert_element_type.12.taps_ref
  17.0 0.0 copy-done
  17.0 0.0 copy-start.2
  17.0 1.2 %copy-done.2 = s16[4,288,384]{2,1,0:T(8,128)(2,1)S(1)} copy-done((s16[4,288,384]{2,1,0:T(8,128)(2,1)S(1)}, s16[4,288,384]{2,1,0:T(8,128)(2,1)}, u32[]{:S(2)}) %copy-start.2) | copy-done | bytes 884760
  18.2 55.0 %shard_map.47.image_ref = bf16[4,96,384]{2,1,0:T(8,128)(2,1)S(1)} custom-call(s32[1]{0:T(128)S(6)} %copy.8.freq_ref, bf16[2,1,2,384,384]{4,3,2,1,0:T(8,128)(2,1)S(1)} %copy-done, s16[4,288,384]{2,1,0:T(8,128)(2,1)S(1)} %copy-done.2, f32[4,64,128]{2,1,0:T(8,128)S(1)} %convert_element_type.12.taps_ref), custom_call_target="tpu_custom_call" | custom-call | tf_op jit(solution)/shard_map/pallas_call | solution.py:251
  73.1 0.0 copy-start.1
  73.2 0.7 copy-done.1
  73.9 18.7 %shard_map.48 = f32[1,96,384]{2,1,0:T(8,128)} custom-call(bf16[4,96,384]{2,1,0:T(8,128)(2,1)} %copy-done.1), custom_call_target="tpu_custom_call" | custom-call | tf_op jit(solution)/shard_map/pallas_call | solution.py:319
  92.6 1.6 %copy.9 = f32[1,96,384]{2,1,0:T(8,128)} copy(f32[1,96,384]{2,1,0:T(8,128)} %shard_map.48) | data formatting | bytes 294912
Async XLA Ops:
  0.0 17.0 %copy-start = (bf16[2,1,2,384,384]{4,3,2,1,0:T(8,128)(2,1)S(1)}, bf16[2,1,2,384,384]{4,3,2,1,0:T(8,128)(2,1)}, u32[]{:S(2)}) copy-start(bf16[2,1,2,384,384]{4,3,2,1,0:T(8,128)(2,1)} %surface_ref.1) | copy-start | bytes 3538948
  17.0 1.2 %copy-start.2 = (s16[4,288,384]{2,1,0:T(8,128)(2,1)S(1)}, s16[4,288,384]{2,1,0:T(8,128)(2,1)}, u32[]{:S(2)}) copy-start(s16[4,288,384]{2,1,0:T(8,128)(2,1)} %get-tuple-element.7.slow_ref) | copy-start | bytes 2654212
  73.1 0.7 copy-start.1

commit v2 on v0

--- a/solution.py
+++ b/solution.py
@@ -1,8 +1,11 @@
+import functools
 import math
 
 import jax
 import jax.numpy as jnp
 from jax import lax
+from jax.experimental import pallas as pl
+from jax.experimental.pallas import tpu as pltpu
 from jax.sharding import PartitionSpec as P
 
 
@@ -55,7 +58,7 @@
     )
 
 
-def on_device(surface, kernels, slowness, freq_index):
+def on_device_general(surface, kernels, slowness, freq_index):
     depth_count = lax.axis_size("depth")
     position = lax.axis_index("depth")
     cells_x = surface.shape[3]
@@ -80,6 +83,245 @@
     return summed * (1.0 / math.sqrt(surface.shape[1] * lax.axis_size("freq")))
 
 
+MESH = pl.DeviceIdType.MESH
+VMEM = pl.BlockSpec(memory_space=pltpu.VMEM)
+SCALE = 32767.0 / 0.02
+
+
+def window(position, rows, cells, margin):
+    length = min(cells, rows + 2 * margin)
+    start = jnp.clip(position * rows - margin, 0, cells - length)
+    offset = start - position * rows + 2 * margin
+    return pl.multiple_of(start, 16), pl.multiple_of(offset, 16), length
+
+
+def sine_cosine(phase):
+    quarter = phase * 0.25
+    sq = quarter * quarter
+    sine = quarter * (1.0 + sq * (-1 / 6 + sq * (1 / 120 + sq * (-1 / 5040 + sq * (1 / 362880 - sq * (1 / 39916800))))))
+    cosine = 1.0 + sq * (-0.5 + sq * (1 / 24 + sq * (-1 / 720 + sq * (1 / 40320 - sq * (1 / 3628800)))))
+    for _ in range(2):
+        sine, cosine = 2.0 * sine * cosine, 1.0 - 2.0 * sine * sine
+    return sine, cosine
+
+
+def tiles_of(total):
+    if total <= 96:
+        return [(0, total)]
+    first = total // 2 // 16 * 16
+    return [(0, first), (first, -(-(total - first) // 16) * 16)]
+
+
+def march_kernel(depth_count, rows, reach, factor, freq_ref, surface_ref, slow_ref, taps_ref, out_ref,
+                 wave0, wave1, band, patches, conv_ref, corr, slow_all, taps_all, image, slots,
+                 sems, local, send, recv, image_send, image_recv):
+    me = lax.axis_index("depth")
+    freq_at = lax.axis_index("freq")
+    count = depth_count
+    margin = depth_count * reach
+    cells = surface_ref.shape[3]
+    cols = surface_ref.shape[4]
+    width = 2 * reach + 1
+    waves = (wave0, wave1)
+
+    barrier = pltpu.get_barrier_semaphore()
+    for step in range(1, count):
+        other = lax.rem(me + step, count)
+        pl.semaphore_signal(barrier, inc=1, device_id={"depth": other}, device_id_type=MESH)
+    for k in range(count):
+        @pl.when((me != freq_at) | (k != freq_at))
+        def _():
+            pl.semaphore_signal(barrier, inc=1, device_id={"depth": freq_at, "freq": k}, device_id_type=MESH)
+    pl.semaphore_wait(barrier, 2 * count - 1 - (me == freq_at).astype(jnp.int32))
+
+    tap_copies = []
+    slow_copies = []
+    for step in range(1, count):
+        other = lax.rem(me + step, count)
+        start, offset, length = window(other, rows, cells, margin)
+        tap_copies.append(pltpu.make_async_remote_copy(
+            src_ref=taps_ref, dst_ref=taps_all.at[me],
+            send_sem=send.at[0, step - 1], recv_sem=recv.at[0, step - 1],
+            device_id={"depth": other}, device_id_type=MESH))
+        slow_copies.append(pltpu.make_async_remote_copy(
+            src_ref=slow_ref.at[pl.ds(start, length)],
+            dst_ref=slow_all.at[me, pl.ds(offset, length)],
+            send_sem=send.at[1, step - 1], recv_sem=recv.at[1, step - 1],
+            device_id={"depth": other}, device_id_type=MESH))
+    start, offset, length = window(me, rows, cells, margin)
+    tap_copies.append(pltpu.make_async_copy(taps_ref, taps_all.at[me], local.at[0]))
+    slow_copies.append(pltpu.make_async_copy(
+        slow_ref.at[pl.ds(start, length)], slow_all.at[me, pl.ds(offset, length)], local.at[1]))
+    for copy in tap_copies + slow_copies:
+        copy.start()
+
+    wave0[...] = jnp.zeros_like(wave0)
+    copies = [
+        pltpu.make_async_copy(
+            surface_ref.at[w, 0, c, pl.ds(start, length)],
+            wave0.at[w, c, pl.ds(offset, length), pl.ds(0, cols)],
+            sems.at[w, c])
+        for w in range(2) for c in range(2)
+    ]
+    for copy in copies:
+        copy.start()
+    wave1[:, :, :, cols:] = jnp.zeros(wave1.shape[:3] + (128,), wave1.dtype)
+    top = rows + 2 * margin
+    patches[:, top:] = jnp.zeros((2 * width, patches.shape[1] - top, 2 * cols), patches.dtype)
+    for copy in copies:
+        copy.wait()
+
+    freq = freq_ref[0].astype(jnp.float32) * (1.0 / SCALE)
+
+    def outgoing(z):
+        return pltpu.make_async_remote_copy(
+            src_ref=image.at[z], dst_ref=slots.at[freq_at],
+            send_sem=image_send.at[z], recv_sem=image_recv.at[freq_at],
+            device_id={"depth": z, "freq": me}, device_id_type=MESH)
+
+    def incoming(k):
+        return pltpu.make_async_remote_copy(
+            src_ref=image.at[k], dst_ref=slots.at[k],
+            send_sem=image_send.at[k], recv_sem=image_recv.at[k],
+            device_id={"depth": k, "freq": me}, device_id_type=MESH)
+
+    for z in range(count):
+        source, target = waves[z % 2], waves[(z + 1) % 2]
+        base = margin if z == 0 else 0
+        shift = reach * (z + 1)
+        total = rows + 2 * reach * (count - 1 - z)
+        needed = -(-(total + 2 * reach) // 16) * 16
+
+        @pl.loop(0, 2)
+        def _(c):
+            for w in range(2):
+                for low in range(0, needed, 64):
+                    size = min(64, needed - low)
+                    block = source[w, c, base + low : base + low + size]
+                    for b in range(width):
+                        moved = pltpu.roll(block, (reach - b) % (cols + 128), 1)
+                        patches[2 * b + c, low : low + size, cols * w : cols * w + cols] = moved[:, :cols]
+
+        if z == 0:
+            for copy in tap_copies:
+                copy.wait()
+
+        @pl.loop(0, width, unroll=5)
+        def _(b):
+            parts = []
+            for k in range(2):
+                line = jnp.broadcast_to(taps_all[z, pl.ds(32 * k + b, 1)], (112, 128))
+                parts.append(pltpu.roll(line, 0, 1, stride=1, stride_axis=0))
+            real, imag = parts
+            low, high = pl.ds(pl.multiple_of(256 * b, 256), 128), pl.ds(pl.multiple_of(256 * b + 128, 128), 128)
+            band[0, :, low] = real.astype(jnp.bfloat16)
+            band[0, :, high] = (-imag).astype(jnp.bfloat16)
+            band[1, :, low] = imag.astype(jnp.bfloat16)
+            band[1, :, high] = real.astype(jnp.bfloat16)
+
+        for at, size in tiles_of(total):
+            total_ref = conv_ref.at[pl.ds(0, 2 * size)]
+            total_ref[...] = jnp.zeros((2 * size, 2 * cols), jnp.float32)
+
+            @pl.loop(0, width // 5)
+            def _(g):
+                deep = pl.ds(pl.multiple_of(1280 * g, 1280), 1280)
+                lhs = jnp.concatenate([band[0, :size, deep], band[1, :size, deep]], 0)
+                rhs = patches[pl.ds(10 * g, 10), at : at + 128].reshape(1280, 2 * cols)
+                total_ref[...] += jnp.dot(lhs, rhs, preferred_element_type=jnp.float32)
+
+            if z == 0 and at == 0:
+                for copy in slow_copies:
+                    copy.wait()
+            phase = slow_all[z, margin + shift + at : margin + shift + at + size].astype(jnp.int32).astype(jnp.float32) * freq
+            sine, cosine = sine_cosine(phase)
+            line = lax.broadcasted_iota(jnp.int32, (size, cols), 0) + (me * rows - margin + shift + at)
+            inside = (line >= 0) & (line < cells)
+            kept = []
+            for w in range(2):
+                real = total_ref[:size, cols * w : cols * w + cols]
+                imag = total_ref[size:, cols * w : cols * w + cols]
+                for c, value in enumerate((real * cosine - imag * sine, real * sine + imag * cosine)):
+                    value = jnp.where(inside, value, 0.0).astype(jnp.bfloat16)
+                    kept.append(value.astype(jnp.float32))
+                    if z + 1 < count:
+                        target[w, c, at : at + size, :cols] = value
+            corr[at : at + size] = (kept[0] * kept[2] + kept[1] * kept[3]) * factor
+        image[z] = corr[margin - shift : margin - shift + rows].astype(image.dtype)
+
+        @pl.when((me != freq_at) | (z != me))
+        def _():
+            outgoing(z).start()
+
+    own = pltpu.make_async_copy(image.at[me], slots.at[freq_at], local.at[2])
+
+    @pl.when(me == freq_at)
+    def _():
+        own.start()
+        own.wait()
+
+    for k in range(count):
+        @pl.when((me != freq_at) | (k != freq_at))
+        def _():
+            incoming(k).wait_recv()
+    result = slots[0].astype(jnp.float32)
+    for k in range(1, count):
+        result = result + slots[k].astype(jnp.float32)
+    out_ref[0] = result
+    for k in range(count):
+        @pl.when((me != freq_at) | (k != me))
+        def _():
+            outgoing(k).wait_send()
+
+
+def march(freq, surface, slow, taps, depth_count, rows, reach, factor):
+    cols = surface.shape[4]
+    width = 2 * reach + 1
+    frame = rows + 4 * depth_count * reach
+    peers = depth_count - 1
+    return pl.pallas_call(
+        functools.partial(march_kernel, depth_count, rows, reach, factor),
+        out_shape=jax.ShapeDtypeStruct((1, rows, cols), jnp.float32),
+        in_specs=[pl.BlockSpec(memory_space=pltpu.SMEM), pl.BlockSpec(memory_space=pl.ANY), VMEM, VMEM],
+        out_specs=VMEM,
+        scratch_shapes=[
+            pltpu.VMEM((2, 2, frame, cols + 128), jnp.bfloat16),
+            pltpu.VMEM((2, 2, frame, cols + 128), jnp.bfloat16),
+            pltpu.VMEM((2, 112, 256 * width), jnp.bfloat16),
+            pltpu.VMEM((2 * width, 208, 2 * cols), jnp.bfloat16),
+            pltpu.VMEM((192, 2 * cols), jnp.float32),
+            pltpu.VMEM((192, cols), jnp.float32),
+            pltpu.VMEM((depth_count, frame, cols), slow.dtype),
+            pltpu.VMEM((depth_count,) + taps.shape, taps.dtype),
+            pltpu.VMEM((depth_count, rows, cols), jnp.bfloat16),
+            pltpu.VMEM((depth_count, rows, cols), jnp.bfloat16),
+            pltpu.SemaphoreType.DMA((2, 2)),
+            pltpu.SemaphoreType.DMA((3,)),
+            pltpu.SemaphoreType.DMA((2, peers)),
+            pltpu.SemaphoreType.DMA((2, peers)),
+            pltpu.SemaphoreType.DMA((depth_count,)),
+            pltpu.SemaphoreType.DMA((depth_count,)),
+        ],
+        compiler_params=pltpu.CompilerParams(collective_id=0, has_side_effects=True, vmem_limit_bytes=48 << 20),
+    )(freq, surface, slow, taps)
+
+
+def on_device_fused(surface, kernels, slowness, freq_index):
+    depth_count = lax.axis_size("depth")
+    rows = surface.shape[3] // depth_count
+    width = kernels.shape[-1]
+    reach = (width - 1) // 2
+    taps = jnp.pad(jnp.swapaxes(kernels[0, 0], 1, 2), ((0, 0), (0, 32 - width), (0, 128 - width)))
+    taps = taps.reshape(64, 128).astype(jnp.float32)
+    slow = jnp.round(slowness[0] * SCALE).astype(jnp.int16)
+    factor = 1.0 / math.sqrt(lax.axis_size("freq"))
+    return march(freq_index, surface, slow, taps, depth_count, rows, reach, factor)
+
+
+def fits(mesh):
+    return mesh.shape["depth"] == 4 and mesh.shape["freq"] == 4
+
+
 def solution(mesh):
     in_specs = (
         P("shots", "freq", None, None, None),
@@ -88,6 +330,7 @@
         P("freq"),
     )
     out_specs = P(("shots", "depth"), "freq", None)
+    body = on_device_fused if fits(mesh) else on_device_general
     return jax.shard_map(
-        on_device, mesh=mesh, in_specs=in_specs, out_specs=out_specs, check_vma=False
-    )
+        body, mesh=mesh, in_specs=in_specs, out_specs=out_specs, check_vma=False
+    )

time: 143 us -> 55.3 us (0.39)
  the two profiles are of different devices: /device:TPU:0 before, /device:TPU:3 now
where the time goes in v2:
time: 55.3 us; the launch traced here: 55.1 us
  Pallas kernels  50.4 us (91%)
  local copies, waits for them, and re-layouts  2.76 us (5%)
  other arithmetic  1.17 us (2%)
  between operations  0.68 us (1%)
    pallas_call x1, Pallas kernels, march(): pl.pallas_call(functools.partial(march_kernel, depth_count, rows, reach,...  50.4 us
    unnamed x4, local copies, waits for them, and re-layouts  2.75 us
    convert_element_type x1, other arithmetic, on_device_fused(): slow = jnp.round(slowness[0] * SCALE).astype(jnp.int16)  1.16 us

profile of v2, /device:TPU:3, one launch (start us, length us, event | category | flops | bytes accessed | tf_op | source)
XLA Modules:
  0.0 55.1 jit_solution(3429435221497626759)
XLA Ops:
  0.7 0.8 %copy.6 = bf16[1,1,2,25,25]{3,4,2,1,0:T(8,128)(2,1)S(1)} copy(bf16[1,1,2,25,25]{4,2,3,1,0:T(2,128)(2,1)} %param.5) | data formatting | bytes 5000 | tf_op args[1]
  1.5 1.2 %fusion.slow_ref = s16[384,384]{1,0:T(8,128)(2,1)S(1)} fusion(f32[1,384,384]{2,1,0:T(8,128)} %param.6), kind=kLoop, calls=%fused_computation.1 | loop fusion | flops 442368 | bytes 884736 | tf_op jit(solution)/shard_map/convert_element_type | solution.py:316
  2.7 0.0 copy-start
  2.7 1.3 %copy-done = bf16[2,1,2,384,384]{4,3,2,1,0:T(8,128)(2,1)S(1)} copy-done((bf16[2,1,2,384,384]{4,3,2,1,0:T(8,128)(2,1)S(1)}, bf16[2,1,2,384,384]{4,3,2,1,0:T(8,128)(2,1)}, u32[]{:S(2)}) %copy-start) | copy-done | bytes 1179672
  3.9 50.4 %shard_map.46 = f32[1,96,384]{2,1,0:T(8,128)S(1)} custom-call(s32[1]{0:T(128)S(6)} %copy.8.freq_ref, bf16[2,1,2,384,384]{4,3,2,1,0:T(8,128)(2,1)S(1)} %copy-done, s16[384,384]{1,0:T(8,128)(2,1)S(1)} %fusion.slow_ref, f32[64,128]{1,0:T(8,128)S(1)} %bitcast_convert_fusion.taps_ref), custom_call_target="tpu_custom_call" | custom-call | tf_op jit(solution)/shard_map/pallas_call | solution.py:282
  54.4 0.7 %copy.9 = f32[1,96,384]{2,1,0:T(8,128)} copy(f32[1,96,384]{2,1,0:T(8,128)S(1)} %shard_map.46) | data formatting | bytes 294912
  (2 shorter events, 0.0 us)
Async XLA Ops:
  2.7 1.3 %copy-start = (bf16[2,1,2,384,384]{4,3,2,1,0:T(8,128)(2,1)S(1)}, bf16[2,1,2,384,384]{4,3,2,1,0:T(8,128)(2,1)}, u32[]{:S(2)}) copy-start(bf16[2,1,2,384,384]{4,3,2,1,0:T(8,128)(2,1)} %surface_ref.1) | copy-start | bytes 3538948

commit v3 on v2

--- a/solution.py
+++ b/solution.py
@@ -113,7 +113,7 @@
 
 
 def march_kernel(depth_count, rows, reach, factor, freq_ref, surface_ref, slow_ref, taps_ref, out_ref,
-                 wave0, wave1, band, patches, conv_ref, corr, slow_all, taps_all, image, slots,
+                 wave0, wave1, band, even, odd, conv_ref, corr, slow_all, taps_all, image, slots,
                  sems, local, send, recv, image_send, image_recv):
     me = lax.axis_index("depth")
     freq_at = lax.axis_index("freq")
@@ -123,6 +123,7 @@
     cols = surface_ref.shape[4]
     width = 2 * reach + 1
     waves = (wave0, wave1)
+    patches = (even, odd)
 
     barrier = pltpu.get_barrier_semaphore()
     for step in range(1, count):
@@ -167,7 +168,8 @@
         copy.start()
     wave1[:, :, :, cols:] = jnp.zeros(wave1.shape[:3] + (128,), wave1.dtype)
     top = rows + 2 * margin
-    patches[:, top:] = jnp.zeros((2 * width, patches.shape[1] - top, 2 * cols), patches.dtype)
+    for held in patches:
+        held[:, top:] = jnp.zeros((10, held.shape[1] - top, 2 * cols), held.dtype)
     for copy in copies:
         copy.wait()
 
@@ -192,15 +194,18 @@
         total = rows + 2 * reach * (count - 1 - z)
         needed = -(-(total + 2 * reach) // 16) * 16
 
-        @pl.loop(0, 2)
-        def _(c):
-            for w in range(2):
-                for low in range(0, needed, 64):
-                    size = min(64, needed - low)
-                    block = source[w, c, base + low : base + low + size]
-                    for b in range(width):
-                        moved = pltpu.roll(block, (reach - b) % (cols + 128), 1)
-                        patches[2 * b + c, low : low + size, cols * w : cols * w + cols] = moved[:, :cols]
+        def build(group, chunk):
+            held = patches[group % 2]
+            c, w, low = chunk
+            size = min(64, needed - low)
+            block = source[w, c, base + low : base + low + size]
+            for b in range(5):
+                moved = pltpu.roll(block, (reach - 5 * group - b) % (cols + 128), 1)
+                held[2 * b + c, low : low + size, cols * w : cols * w + cols] = moved[:, :cols]
+
+        chunks = [(c, w, low) for c in range(2) for w in range(2) for low in range(0, needed, 64)]
+        for chunk in chunks:
+            build(0, chunk)
 
         if z == 0:
             for copy in tap_copies:
@@ -219,17 +224,28 @@
             band[1, :, low] = imag.astype(jnp.bfloat16)
             band[1, :, high] = real.astype(jnp.bfloat16)
 
-        for at, size in tiles_of(total):
-            total_ref = conv_ref.at[pl.ds(0, 2 * size)]
-            total_ref[...] = jnp.zeros((2 * size, 2 * cols), jnp.float32)
-
-            @pl.loop(0, width // 5)
-            def _(g):
-                deep = pl.ds(pl.multiple_of(1280 * g, 1280), 1280)
+        tiles = tiles_of(total)
+        parts = [(at, size, n) for at, size in tiles for n in range(2 * cols // 256)]
+        for group in range(width // 5):
+            ahead = list(chunks) if group + 1 < width // 5 else []
+            share = -(-len(ahead) // len(parts))
+            for at, size, n in parts:
+                for chunk in ahead[:share]:
+                    build(group + 1, chunk)
+                ahead = ahead[share:]
+                deep = slice(1280 * group, 1280 * group + 1280)
+                across = slice(256 * n, 256 * n + 256)
                 lhs = jnp.concatenate([band[0, :size, deep], band[1, :size, deep]], 0)
-                rhs = patches[pl.ds(10 * g, 10), at : at + 128].reshape(1280, 2 * cols)
-                total_ref[...] += jnp.dot(lhs, rhs, preferred_element_type=jnp.float32)
-
+                rhs = patches[group % 2][:, at : at + 128, across].reshape(1280, 256)
+                product = jnp.dot(lhs, rhs, preferred_element_type=jnp.float32)
+                rows_at = slice(2 * at, 2 * at + 2 * size)
+                if group == 0:
+                    conv_ref[rows_at, across] = product
+                else:
+                    conv_ref[rows_at, across] += product
+
+        for at, size in tiles:
+            total_ref = conv_ref.at[pl.ds(2 * at, 2 * size)]
             if z == 0 and at == 0:
                 for copy in slow_copies:
                     copy.wait()
@@ -288,8 +304,9 @@
             pltpu.VMEM((2, 2, frame, cols + 128), jnp.bfloat16),
             pltpu.VMEM((2, 2, frame, cols + 128), jnp.bfloat16),
             pltpu.VMEM((2, 112, 256 * width), jnp.bfloat16),
-            pltpu.VMEM((2 * width, 208, 2 * cols), jnp.bfloat16),
-            pltpu.VMEM((192, 2 * cols), jnp.float32),
+            pltpu.VMEM((10, 208, 2 * cols), jnp.bfloat16),
+            pltpu.VMEM((10, 208, 2 * cols), jnp.bfloat16),
+            pltpu.VMEM((384, 2 * cols), jnp.float32),
             pltpu.VMEM((192, cols), jnp.float32),
             pltpu.VMEM((depth_count, frame, cols), slow.dtype),
             pltpu.VMEM((depth_count,) + taps.shape, taps.dtype),

time: 55.3 us -> 44.2 us (0.80)
  Pallas kernels: 50.4 us -> 38.9 us
    pallas_call x1, Pallas kernels: 50.4 us -> 38.9 us  [march(): pl.pallas_call(functools.partial(march_kernel, depth_count, rows, reach,...]
where the time goes in v3:
time: 44.2 us; the launch traced here: 43.5 us
  Pallas kernels  38.9 us (88%)
  local copies, waits for them, and re-layouts  2.76 us (6%)
  other arithmetic  1.17 us (3%)
  between operations  0.68 us (2%)
    pallas_call x1, Pallas kernels, march(): pl.pallas_call(functools.partial(march_kernel, depth_count, rows, reach,...  38.9 us
    unnamed x4, local copies, waits for them, and re-layouts  2.75 us
    convert_element_type x1, other arithmetic, on_device_fused(): slow = jnp.round(slowness[0] * SCALE).astype(jnp.int16)  1.16 us

profile of v3, /device:TPU:3, one launch (start us, length us, event | category | flops | bytes accessed | tf_op | source)
XLA Modules:
  0.0 43.5 jit_solution(2203474151606859752)
XLA Ops:
  0.7 0.8 %copy.6 = bf16[1,1,2,25,25]{3,4,2,1,0:T(8,128)(2,1)S(1)} copy(bf16[1,1,2,25,25]{4,2,3,1,0:T(2,128)(2,1)} %param.5) | data formatting | bytes 5000 | tf_op args[1]
  1.5 1.2 %fusion.slow_ref = s16[384,384]{1,0:T(8,128)(2,1)S(1)} fusion(f32[1,384,384]{2,1,0:T(8,128)} %param.6), kind=kLoop, calls=%fused_computation.1 | loop fusion | flops 442368 | bytes 884736 | tf_op jit(solution)/shard_map/convert_element_type | solution.py:333
  2.7 0.0 copy-start
  2.7 1.3 %copy-done = bf16[2,1,2,384,384]{4,3,2,1,0:T(8,128)(2,1)S(1)} copy-done((bf16[2,1,2,384,384]{4,3,2,1,0:T(8,128)(2,1)S(1)}, bf16[2,1,2,384,384]{4,3,2,1,0:T(8,128)(2,1)}, u32[]{:S(2)}) %copy-start) | copy-done | bytes 1179672
  3.9 38.9 %shard_map.46 = f32[1,96,384]{2,1,0:T(8,128)S(1)} custom-call(s32[1]{0:T(128)S(6)} %copy.8.freq_ref, bf16[2,1,2,384,384]{4,3,2,1,0:T(8,128)(2,1)S(1)} %copy-done, s16[384,384]{1,0:T(8,128)(2,1)S(1)} %fusion.slow_ref, f32[64,128]{1,0:T(8,128)S(1)} %bitcast_convert_fusion.taps_ref), custom_call_target="tpu_custom_call" | custom-call | tf_op jit(solution)/shard_map/pallas_call | solution.py:298
  42.9 0.7 %copy.9 = f32[1,96,384]{2,1,0:T(8,128)} copy(f32[1,96,384]{2,1,0:T(8,128)S(1)} %shard_map.46) | data formatting | bytes 294912
  (2 shorter events, 0.0 us)
Async XLA Ops:
  2.7 1.3 %copy-start = (bf16[2,1,2,384,384]{4,3,2,1,0:T(8,128)(2,1)S(1)}, bf16[2,1,2,384,384]{4,3,2,1,0:T(8,128)(2,1)}, u32[]{:S(2)}) copy-start(bf16[2,1,2,384,384]{4,3,2,1,0:T(8,128)(2,1)} %surface_ref.1) | copy-start | bytes 3538948

commit v4 on v3

--- a/solution.py
+++ b/solution.py
@@ -211,7 +211,7 @@
             for copy in tap_copies:
                 copy.wait()
 
-        @pl.loop(0, width, unroll=5)
+        @pl.loop(0, width, unroll=width)
         def _(b):
             parts = []
             for k in range(2):

time: 44.2 us -> 40.7 us (0.921)
  Pallas kernels: 38.9 us -> 35.4 us
    pallas_call x1, Pallas kernels: 38.9 us -> 35.4 us  [march(): pl.pallas_call(functools.partial(march_kernel, depth_count, rows, reach,...]
where the time goes in v4:
time: 40.7 us; the launch traced here: 40 us
  Pallas kernels  35.4 us (87%)
  local copies, waits for them, and re-layouts  2.76 us (7%)
  other arithmetic  1.17 us (3%)
  between operations  0.68 us (2%)
    pallas_call x1, Pallas kernels, march(): pl.pallas_call(functools.partial(march_kernel, depth_count, rows, reach,...  35.4 us
    unnamed x4, local copies, waits for them, and re-layouts  2.75 us
    convert_element_type x1, other arithmetic, on_device_fused(): slow = jnp.round(slowness[0] * SCALE).astype(jnp.int16)  1.16 us

profile of v4, /device:TPU:3, one launch (start us, length us, event | category | flops | bytes accessed | tf_op | source)
XLA Modules:
  0.0 40.0 jit_solution(10453540703494059487)
XLA Ops:
  0.7 0.8 %copy.6 = bf16[1,1,2,25,25]{3,4,2,1,0:T(8,128)(2,1)S(1)} copy(bf16[1,1,2,25,25]{4,2,3,1,0:T(2,128)(2,1)} %param.5) | data formatting | bytes 5000 | tf_op args[1]
  1.5 1.2 %fusion.slow_ref = s16[384,384]{1,0:T(8,128)(2,1)S(1)} fusion(f32[1,384,384]{2,1,0:T(8,128)} %param.6), kind=kLoop, calls=%fused_computation.1 | loop fusion | flops 442368 | bytes 884736 | tf_op jit(solution)/shard_map/convert_element_type | solution.py:333
  2.7 0.0 copy-start
  2.7 1.3 %copy-done = bf16[2,1,2,384,384]{4,3,2,1,0:T(8,128)(2,1)S(1)} copy-done((bf16[2,1,2,384,384]{4,3,2,1,0:T(8,128)(2,1)S(1)}, bf16[2,1,2,384,384]{4,3,2,1,0:T(8,128)(2,1)}, u32[]{:S(2)}) %copy-start) | copy-done | bytes 1179672
  3.9 35.4 %shard_map.46 = f32[1,96,384]{2,1,0:T(8,128)S(1)} custom-call(s32[1]{0:T(128)S(6)} %copy.8.freq_ref, bf16[2,1,2,384,384]{4,3,2,1,0:T(8,128)(2,1)S(1)} %copy-done, s16[384,384]{1,0:T(8,128)(2,1)S(1)} %fusion.slow_ref, f32[64,128]{1,0:T(8,128)S(1)} %bitcast_convert_fusion.taps_ref), custom_call_target="tpu_custom_call" | custom-call | tf_op jit(solution)/shard_map/pallas_call | solution.py:298
  39.4 0.7 %copy.9 = f32[1,96,384]{2,1,0:T(8,128)} copy(f32[1,96,384]{2,1,0:T(8,128)S(1)} %shard_map.46) | data formatting | bytes 294912
  (2 shorter events, 0.0 us)
Async XLA Ops:
  2.7 1.3 %copy-start = (bf16[2,1,2,384,384]{4,3,2,1,0:T(8,128)(2,1)S(1)}, bf16[2,1,2,384,384]{4,3,2,1,0:T(8,128)(2,1)}, u32[]{:S(2)}) copy-start(bf16[2,1,2,384,384]{4,3,2,1,0:T(8,128)(2,1)} %surface_ref.1) | copy-start | bytes 3538948
